TPU v7x, 32 devices: a whole 2x2x4 slice. The times are simulated.
32 devices in a mesh: replica: 8 (over z, core), shard: 4 (over y, x).
Axes of the slice: x: 2, y: 2, z: 4, core: 2. Of those that a mesh axis runs over, the one named last changes fastest.
Arguments:
- local_weights: bfloat16 [8, 8192, 512], P('replica', 'shard'), may hold values from -1.3258252 to 1.3258252
- outer_base: bfloat16 [8192, 512], P('shard'), may hold values from -0.0625 to 0.0625
- momentum: bfloat16 [8192, 512], P('shard', 'replica'), may hold values from -0.06591797 to 0.06591797
- error_feedback: bfloat16 [8, 8192, 512], P('replica', 'shard'), may hold values from -0.032958984 to 0.032958984
- q_start: float32 [512, 32], replicated, may hold values from -6 to 6
- tokens: bfloat16 [8, 512, 8192], P('replica', None, 'shard'), may hold values from -6 to 6
Outputs:
- new_base: bfloat16 [8192, 512], P('shard')
- new_momentum: bfloat16 [8192, 512], P('shard', 'replica')
- new_error: bfloat16 [8, 8192, 512], P('replica', 'shard')
- key_rows: bfloat16 [8, 512, 512], P('replica', 'shard')
All inputs are finite; a program needn't handle non-finite values.
Results may differ from a plain program's by a relative error of at most 0.0065.
Values may be sent and summed in bfloat16 or wider, within the bound.
A program may use at most 64 MiB of HBM per device.

v0:
```python
import jax
import jax.numpy as jnp
from jax import lax
from jax.sharding import PartitionSpec as P

outer_mu = 0.9
outer_rate = 0.7


def on_device(local_weights, outer_base, momentum, error_feedback, q_start, tokens):
    highest = lax.Precision.HIGHEST
    replicas = lax.axis_size("replica")
    own_columns = momentum.shape[1]
    full_momentum = lax.all_gather(momentum, "replica", axis=1, tiled=True)
    pseudo = (
        outer_base.astype(jnp.float32)
        - local_weights[0].astype(jnp.float32)
        + error_feedback[0].astype(jnp.float32)
    )
    p_local = jnp.dot(pseudo, q_start, precision=highest)
    p_mean = lax.psum(p_local, "replica") / replicas
    own_gram = jnp.dot(p_mean.T, p_mean, precision=highest)
    gram_sum = lax.psum(own_gram, "shard")
    factor_low = jnp.linalg.cholesky(gram_sum)
    basis = jax.scipy.linalg.solve_triangular(factor_low, p_mean.T, lower=True).T
    q_raw = jnp.dot(pseudo.T, basis, precision=highest)
    q_mean = lax.psum(q_raw, ("replica", "shard")) / replicas
    update = jnp.dot(basis, q_mean.T, precision=highest)
    new_error = (pseudo - update).astype(jnp.bfloat16)[None]
    moment = outer_mu * full_momentum.astype(jnp.float32) + update
    new_base = (outer_base.astype(jnp.float32) - outer_rate * (outer_mu * moment + update)).astype(
        jnp.bfloat16
    )
    first_column = lax.axis_index("replica") * own_columns
    new_momentum = lax.dynamic_slice_in_dim(moment, first_column, own_columns, 1).astype(
        jnp.bfloat16
    )
    own_tokens = tokens[0]
    key_sum = lax.psum_scatter(
        jnp.dot(own_tokens, new_base, preferred_element_type=jnp.float32),
        "shard",
        scatter_dimension=0,
        tiled=True,
    )
    key_rows = key_sum.astype(jnp.bfloat16)[None]
    return (new_base, new_momentum, new_error, key_rows)


def solution(mesh):
    in_specs = (
        P("replica", "shard", None),
        P("shard", None),
        P("shard", "replica"),
        P("replica", "shard", None),
        P(),
        P("replica", None, "shard"),
    )
    out_specs = (
        P("shard", None),
        P("shard", "replica"),
        P("replica", "shard", None),
        P("replica", "shard", None),
    )
    return jax.shard_map(
        on_device, mesh=mesh, in_specs=in_specs, out_specs=out_specs, check_vma=False
    )
```

profile of v0, /device:TPU:0, one launch (start us, length us, event | category | flops | bytes accessed | tf_op | source)
XLA Modules:
  0.0 319.2 jit_solution(3947755793024692435)
XLA Ops:
  7.2 0.0 copy-start
  7.2 0.0 all-reduce.3.cloned.1.call-start
  7.2 4.1 %copy.10 = bf16[2048,512]{0,1:T(8,128)(2,1)} copy(bf16[2048,512]{1,0:T(8,128)(2,1)} %param.7) | data formatting | bytes 4194304 | tf_op args[1]
  11.3 4.0 %copy.11 = bf16[1,2048,512]{1,2,0:T(8,128)(2,1)} copy(bf16[1,2048,512]{2,1,0:T(8,128)(2,1)} %param.6) | data formatting | bytes 4194304 | tf_op args[0]
  15.3 0.0 copy-start.6
  15.3 3.9 %copy.12 = bf16[1,2048,512]{1,2,0:T(8,128)(2,1)} copy(bf16[1,2048,512]{2,1,0:T(8,128)(2,1)} %param.9) | data formatting | bytes 4194304 | tf_op args[3]
  19.2 0.0 copy-done.6
  19.2 6.8 %fusion.10 = f32[2048,32]{0,1:T(8,128)} fusion(f32[512,32]{0,1:T(8,128)S(1)} %copy-done.6, bf16[2048,512]{0,1:T(8,128)(2,1)} %copy.10, bf16[1,2048,512]{1,2,0:T(8,128)(2,1)} %copy.12, bf16[1,2048,512]{1,2,0:T(8,128)(2,1)} %copy.11), kind=kOutput, calls=%fused_computation.11 | convolution fusion | flops 407896064 | bytes 6619136 | tf_op jit(solution)/shard_map/dot_general | solution.py:20
  26.0 0.0 all-reduce.3.cloned.1.call-update
  26.0 0.0 all-reduce.5.cloned.1.call-start
  26.1 58.3 %all-reduce.3.cloned.1.call-done = f32[2048,32]{0,1:T(8,128)} async-done(((f32[2048,32]{0,1:T(8,128)}), f32[2048,32]{0,1:T(8,128)}) %all-reduce.3.cloned.1.call-update) | async-done | bytes 262160 | tf_op jit(solution)/shard_map/psum | solution.py:21
  84.3 1.4 fusion.16
  85.7 16.0 %psum.22 = f32[32,32]{0,1:T(8,128)S(1)} all-reduce(f32[32,32]{0,1:T(8,128)S(1)} %fusion.16), channel_id=1, replica_groups=mesh['replica'=8,'shard'=4] {'shard'}, use_global_device_ids=true, to_apply=%region_1.0 | all-reduce | flops 1024 | bytes 8192 | tf_op jit(solution)/shard_map/psum | solution.py:23
  101.7 0.1 copy.14
  101.8 2.9 cholesky.16
  104.7 0.6 compare_reduce_fusion
  105.4 0.7 fusion.21
  106.0 2.4 custom-call.7
  108.4 1.4 fusion.14
  109.8 6.4 %fusion.8 = f32[512,32]{1,0:T(8,128)} fusion(f32[32,2048]{1,0:T(8,128)S(1)} %fusion.14, bf16[2048,512]{0,1:T(8,128)(2,1)} %copy.10, bf16[1,2048,512]{1,2,0:T(8,128)(2,1)} %copy.12, bf16[1,2048,512]{1,2,0:T(8,128)(2,1)} %copy.11), kind=kOutput, calls=%fused_computation.10 | convolution fusion | flops 407896064 | bytes 6619136 | tf_op jit(solution)/shard_map/dot_general | solution.py:26
  116.2 0.0 all-reduce.5.cloned.1.call-update
  116.3 0.0 all-gather.2.cloned.1.call-start
  116.3 0.7 all-gather.2.cloned.1.call-update
  117.0 0.2 reduce-scatter.2.cloned.1.call-start
  117.2 123.0 %all-reduce.5.cloned.1.call-done = f32[512,32]{1,0:T(8,128)} async-done(((f32[512,32]{1,0:T(8,128)}), f32[512,32]{1,0:T(8,128)}) %all-reduce.5.cloned.1.call-update) | async-done | bytes 65552 | tf_op jit(solution)/shard_map/psum | solution.py:27
  240.2 29.8 %all-gather.2.cloned.1.call-done = bf16[2048,512]{0,1:T(8,128)(2,1)} async-done(((bf16[2048,64]{0,1:T(8,128)(2,1)}), bf16[2048,512]{0,1:T(8,128)(2,1)}) %all-gather.2.cloned.1.call-update) | async-done | bytes 2097168 | tf_op jit(solution)/shard_map/all_gather | solution.py:14
  270.1 0.0 copy-start.1
  270.1 0.0 copy-start.2
  270.1 0.0 copy-start.3
  270.1 0.0 copy-start.4
  270.1 6.3 %multiply_add_fusion = (bf16[2048,512]{0,1:T(8,128)(2,1)}, f32[2048,512]{0,1:T(8,128)S(1)}) fusion(bf16[2048,512]{0,1:T(8,128)(2,1)} %all-gather.2.cloned.1.call-done, f32[32,2048]{1,0:T(8,128)S(1)} %fusion.14, f32[512,32]{1,0:T(8,128)} %all-reduce.5.cloned.1.call-done), kind=kOutput, calls=%fused_computation.5 | convolution fusion | flops 406863872 | bytes 8716288 | tf_op jit(solution)/shard_map/dot_general | solution.py:28
  276.4 0.0 copy-done.1
  276.4 0.0 copy-done.2
  276.4 0.0 copy-done.3
  276.4 0.0 copy-done.4
  276.4 3.5 %fusion.2 = (bf16[1,2048,512]{1,2,0:T(8,128)(2,1)}, bf16[2048,512]{0,1:T(8,128)(2,1)S(1)}) fusion(f32[2048,512]{0,1:T(8,128)S(1)} %get-tuple-element.11, bf16[1,2048,512]{1,2,0:T(8,128)(2,1)S(1)} %copy-done.3, bf16[1,2048,512]{1,2,0:T(8,128)(2,1)S(1)} %copy-done.2, bf16[2048,512]{0,1:T(8,128)(2,1)S(1)} %copy-done.1, bf16[2048,512]{0,1:T(8,128)(2,1)S(1)} %copy-done.4), kind=kLoop, calls=%fused_computation.6 | loop fusion | flops 15728640 | bytes 16777216 | tf_op jit(solution)/shard_map/broadcast_in_dim | solution.py:29
  279.8 0.0 copy-start.5
  279.9 1.3 copy-done.5
  281.2 0.0 copy-done
  281.2 2.3 fusion.5
  283.4 0.0 reduce-scatter.2.cloned.1.call-update
  283.5 3.9 %copy.15 = bf16[2048,512]{1,0:T(8,128)(2,1)} copy(bf16[2048,512]{0,1:T(8,128)(2,1)} %copy-done.5) | data formatting | bytes 4194304
  287.4 4.0 %copy.16 = bf16[1,2048,512]{2,1,0:T(8,128)(2,1)} copy(bf16[1,2048,512]{1,2,0:T(8,128)(2,1)} %get-tuple-element.8) | data formatting | bytes 4194304
  291.3 1.7 dynamic-slice_convert_fusion
  293.0 17.9 %reduce-scatter.2.cloned.1.call-done = f32[128,512]{0,1:T(8,128)} async-done(((f32[512,512]{0,1:T(8,128)}), f32[128,512]{0,1:T(8,128)}) %reduce-scatter.2.cloned.1.call-update) | async-done | bytes 262160 | tf_op jit(solution)/shard_map/reduce_scatter | solution.py:39
  310.9 1.0 convert_bitcast_fusion
  311.9 0.8 copy.17
  (2 shorter events, 0.0 us)
Async XLA Ops:
  7.2 274.0 %copy-start = (bf16[1,512,2048]{2,1,0:T(8,128)(2,1)S(1)}, bf16[1,512,2048]{2,1,0:T(8,128)(2,1)}, u32[]{:S(2)}) copy-start(bf16[1,512,2048]{2,1,0:T(8,128)(2,1)} %param.11) | copy-start | bytes 6291460
  7.2 77.1 %all-reduce.3.cloned.1.call-start = ((), (), s32[]{:S(2)}) async-start(), calls=%async_computation.2 | async-start | bytes 524288 | tf_op jit(solution)/shard_map/psum | solution.py:21
  15.3 3.9 %copy-start.6 = (f32[512,32]{0,1:T(8,128)S(1)}, f32[512,32]{0,1:T(8,128)}, u32[]{:S(2)}) copy-start(f32[512,32]{0,1:T(8,128)} %param.10) | copy-start | bytes 196612
  26.0 214.2 %all-reduce.5.cloned.1.call-start = ((), (), s32[]{:S(2)}) async-start(), calls=%async_computation.3 | async-start | bytes 524288 | tf_op jit(solution)/shard_map/psum | solution.py:27
  116.3 153.8 %all-gather.2.cloned.1.call-start = ((), (), s32[]{:S(2)}) async-start(), calls=%async_computation.1 | async-start | bytes 2359296 | tf_op jit(solution)/shard_map/all_gather | solution.py:14
  117.0 193.9 %reduce-scatter.2.cloned.1.call-start = ((), (), s32[]{:S(2)}) async-start(), calls=%async_computation.4 | async-start | bytes 1310720 | tf_op jit(solution)/shard_map/reduce_scatter | solution.py:39
  270.1 6.3 %copy-start.1 = (bf16[2048,512]{0,1:T(8,128)(2,1)S(1)}, bf16[2048,512]{0,1:T(8,128)(2,1)}, u32[]{:S(2)}) copy-start(bf16[2048,512]{0,1:T(8,128)(2,1)} %copy.10) | copy-start | bytes 6291460
  270.1 6.3 %copy-start.2 = (bf16[1,2048,512]{1,2,0:T(8,128)(2,1)S(1)}, bf16[1,2048,512]{1,2,0:T(8,128)(2,1)}, u32[]{:S(2)}) copy-start(bf16[1,2048,512]{1,2,0:T(8,128)(2,1)} %copy.11) | copy-start | bytes 6291460
  270.1 6.3 %copy-start.3 = (bf16[1,2048,512]{1,2,0:T(8,128)(2,1)S(1)}, bf16[1,2048,512]{1,2,0:T(8,128)(2,1)}, u32[]{:S(2)}) copy-start(bf16[1,2048,512]{1,2,0:T(8,128)(2,1)} %copy.12) | copy-start | bytes 6291460
  270.1 6.3 %copy-start.4 = (bf16[2048,512]{0,1:T(8,128)(2,1)S(1)}, bf16[2048,512]{0,1:T(8,128)(2,1)}, u32[]{:S(2)}) copy-start(bf16[2048,512]{0,1:T(8,128)(2,1)} %all-gather.2.cloned.1.call-done) | copy-start | bytes 6291460
  279.8 1.3 copy-start.5
Sparse Core Ops, SparseCore 0:
  26.1 58.1 all-reduce.2
  116.4 123.7 all-reduce.4
  241.8 28.1 all-gather.1
  283.6 27.3 reduce-scatter.1
where the time goes:
time: 320 us; the launch traced here: 319 us
  waiting for transfers between devices  230 us (72%)
  matrix products  24.5 us (8%)
  local copies, waits for them, and re-layouts  23.7 us (7%)
  blocking collectives  16 us (5%)
  between operations  13.8 us (4%)
  other arithmetic  11.1 us (3%)
    psum x1, waiting for transfers between devices, on_device(): q_mean = lax.psum(q_raw, ('replica', 'shard')) / replicas  123 us
    psum x1, waiting for transfers between devices, on_device(): p_mean = lax.psum(p_local, 'replica') / replicas  58.3 us
    all_gather x1, waiting for transfers between devices, on_device(): full_momentum = lax.all_gather(momentum, 'replica', axis=1, tiled=True)  29.8 us
    unnamed x20, local copies, waits for them, and re-layouts  22 us
    reduce_scatter x1, waiting for transfers between devices, on_device(): lax.psum_scatter(jnp.dot(own_tokens, new_base, preferred_element_type=jnp...  17.9 us
    psum x1, blocking collectives, on_device(): gram_sum = lax.psum(own_gram, 'shard')  16 us
    dot_general x1, matrix products, on_device(): p_local = jnp.dot(pseudo, q_start, precision=highest)  6.77 us
  transfers between devices with their start and end apart: 4, of which 4 were waited for; matrix products, arithmetic and copies ran while one was open for 3% of the time, Pallas kernels for 0%

commit v1 on v0

--- a/solution.py
+++ b/solution.py
@@ -11,7 +11,14 @@
     highest = lax.Precision.HIGHEST
     replicas = lax.axis_size("replica")
     own_columns = momentum.shape[1]
-    full_momentum = lax.all_gather(momentum, "replica", axis=1, tiled=True)
+    ring = [momentum]
+    for hop in range(7):
+        ring.append(lax.ppermute(ring[-1], "replica", [(dev, (dev + 1) % 8) for dev in range(8)]))
+    full_momentum = jnp.roll(
+        jnp.concatenate(ring[::-1], axis=1),
+        (lax.axis_index("replica") + 1) * ring[0].shape[1],
+        axis=1,
+    )
     pseudo = (
         outer_base.astype(jnp.float32)
         - local_weights[0].astype(jnp.float32)

time: 320 us -> 309 us (0.966)
  waiting for transfers between devices: 230 us -> 198 us
  local copies, waits for them, and re-layouts: 23.7 us -> 41.6 us
    all_gather x1 -> x0, waiting for transfers between devices: 29.8 us -> none  [on_device(): full_momentum = lax.all_gather(momentum, 'replica', axis=1, tiled=True)]
    ppermute x0 -> x7, waiting for transfers between devices: none -> 17.4 us  [on_device(): lax.ppermute(ring[-1], 'replica', [(dev, (dev + 1) % 8) for dev in range(...]
    unnamed x20 -> x39, local copies, waits for them, and re-layouts: 22 us -> 39.2 us
    psum x1, waiting for transfers between devices: 123 us -> 106 us  [on_device(): q_mean = lax.psum(q_raw, ('replica', 'shard')) / replicas]
  transfers between devices with their start and end apart: 4 -> 10, of which waited for: 4 -> 8; matrix products, arithmetic and copies ran while one was open for 3% -> 20% of each run, Pallas kernels for 0% -> 0%
where the time goes in v1:
time: 309 us; the launch traced here: 308 us
  waiting for transfers between devices  198 us (64%)
  local copies, waits for them, and re-layouts  41.6 us (13%)
  matrix products  24.5 us (8%)
  blocking collectives  16 us (5%)
  between operations  13.9 us (4%)
  other arithmetic  12.3 us (4%)
    psum x1, waiting for transfers between devices, on_device(): q_mean = lax.psum(q_raw, ('replica', 'shard')) / replicas  106 us
    psum x1, waiting for transfers between devices, on_device(): p_mean = lax.psum(p_local, 'replica') / replicas  56.9 us
    unnamed x39, local copies, waits for them, and re-layouts  39.2 us
    reduce_scatter x1, waiting for transfers between devices, on_device(): lax.psum_scatter(jnp.dot(own_tokens, new_base, preferred_element_type=jnp...  17.6 us
    ppermute x7, waiting for transfers between devices, on_device(): lax.ppermute(ring[-1], 'replica', [(dev, (dev + 1) % 8) for dev in range(...  17.4 us
    psum x1, blocking collectives, on_device(): gram_sum = lax.psum(own_gram, 'shard')  16 us
    dot_general x1, matrix products, on_device(): p_local = jnp.dot(pseudo, q_start, precision=highest)  6.77 us
    dot_general x1, matrix products, on_device(): q_raw = jnp.dot(pseudo.T, basis, precision=highest)  6.39 us
  transfers between devices with their start and end apart: 10, of which 8 were waited for; matrix products, arithmetic and copies ran while one was open for 20% of the time, Pallas kernels for 0%

profile of v1, /device:TPU:0, one launch (start us, length us, event | category | flops | bytes accessed | tf_op | source)
XLA Modules:
  0.0 307.9 jit_solution(5158362055439508418)
XLA Ops:
  7.2 0.0 copy-start
  7.2 0.0 all-reduce.3.cloned.1.call-start
  7.2 0.5 collective-permute-start
  7.8 8.3 %collective-permute-done = bf16[2048,64]{0,1:T(8,128)(2,1)S(1)} collective-permute-done((bf16[2048,64]{0,1:T(8,128)(2,1)}, bf16[2048,64]{0,1:T(8,128)(2,1)S(1)}, u32[]{:S(2)}, u32[]{:S(2)}) %collective-permute-start) | collective-permute-done | bytes 262176 | tf_op jit(solution)/shard_map/ppermute | solution.py:16
  16.1 0.0 collective-permute-start.1
  16.1 4.0 %copy.11 = bf16[1,2048,512]{1,2,0:T(8,128)(2,1)} copy(bf16[1,2048,512]{2,1,0:T(8,128)(2,1)} %param.6) | data formatting | bytes 4194304 | tf_op args[0]
  20.0 3.9 %copy.10 = bf16[2048,512]{0,1:T(8,128)(2,1)} copy(bf16[2048,512]{1,0:T(8,128)(2,1)} %param.7) | data formatting | bytes 4194304 | tf_op args[1]
  24.0 3.9 %copy.12 = bf16[1,2048,512]{1,2,0:T(8,128)(2,1)} copy(bf16[1,2048,512]{2,1,0:T(8,128)(2,1)} %param.9) | data formatting | bytes 4194304 | tf_op args[3]
  27.9 0.0 collective-permute-done.1
  27.9 0.4 collective-permute-start.2
  28.3 6.8 %fusion.10 = f32[2048,32]{0,1:T(8,128)} fusion(f32[512,32]{0,1:T(8,128)S(1)} %copy-done.8, bf16[2048,512]{0,1:T(8,128)(2,1)} %copy.10, bf16[1,2048,512]{1,2,0:T(8,128)(2,1)} %copy.12, bf16[1,2048,512]{1,2,0:T(8,128)(2,1)} %copy.11), kind=kOutput, calls=%fused_computation.11 | convolution fusion | flops 407896064 | bytes 6619136 | tf_op jit(solution)/shard_map/dot_general | solution.py:27
  35.0 0.0 all-reduce.3.cloned.1.call-update
  35.1 0.0 all-reduce.5.cloned.1.call-start
  35.1 0.4 collective-permute-done.2
  35.5 0.0 collective-permute-start.3
  35.5 56.9 %all-reduce.3.cloned.1.call-done = f32[2048,32]{0,1:T(8,128)} async-done(((f32[2048,32]{0,1:T(8,128)}), f32[2048,32]{0,1:T(8,128)}) %all-reduce.3.cloned.1.call-update) | async-done | bytes 262160 | tf_op jit(solution)/shard_map/psum | solution.py:28
  92.3 1.4 fusion.16
  93.7 16.0 %psum.22 = f32[32,32]{0,1:T(8,128)S(1)} all-reduce(f32[32,32]{0,1:T(8,128)S(1)} %fusion.16), channel_id=1, replica_groups=mesh['replica'=8,'shard'=4] {'shard'}, use_global_device_ids=true, to_apply=%region_1.2 | all-reduce | flops 1024 | bytes 8192 | tf_op jit(solution)/shard_map/psum | solution.py:30
  109.7 0.1 copy.14
  109.8 0.0 collective-permute-done.3
  109.8 0.1 collective-permute-start.4
  109.9 2.9 cholesky.16
  112.8 0.6 compare_reduce_fusion
  113.4 4.1 %collective-permute-done.4 = bf16[2048,64]{0,1:T(8,128)(2,1)} collective-permute-done((bf16[2048,64]{0,1:T(8,128)(2,1)S(1)}, bf16[2048,64]{0,1:T(8,128)(2,1)}, u32[]{:S(2)}, u32[]{:S(2)}) %collective-permute-start.4) | collective-permute-done | bytes 262176 | tf_op jit(solution)/shard_map/ppermute | solution.py:16
  117.5 0.0 collective-permute-start.5
  117.5 0.7 fusion.21
  118.2 2.4 custom-call.7
  120.6 1.4 fusion.14
  122.0 0.0 copy-start.5
  122.0 3.4 %collective-permute-done.5 = bf16[2048,64]{0,1:T(8,128)(2,1)} collective-permute-done((bf16[2048,64]{0,1:T(8,128)(2,1)}, bf16[2048,64]{0,1:T(8,128)(2,1)}, u32[]{:S(2)}, u32[]{:S(2)}) %collective-permute-start.5) | collective-permute-done | bytes 262176 | tf_op jit(solution)/shard_map/ppermute | solution.py:16
  125.4 0.0 collective-permute-start.6
  125.4 6.4 %fusion.8 = f32[512,32]{1,0:T(8,128)} fusion(f32[32,2048]{1,0:T(8,128)S(1)} %fusion.14, bf16[2048,512]{0,1:T(8,128)(2,1)} %copy.10, bf16[1,2048,512]{1,2,0:T(8,128)(2,1)} %copy.12, bf16[1,2048,512]{1,2,0:T(8,128)(2,1)} %copy.11), kind=kOutput, calls=%fused_computation.10 | convolution fusion | flops 407896064 | bytes 6619136 | tf_op jit(solution)/shard_map/dot_general | solution.py:33
  131.8 0.0 all-reduce.5.cloned.1.call-update
  131.9 0.2 reduce-scatter.2.cloned.1.call-start
  132.1 0.0 copy-start.7
  132.1 1.3 collective-permute-done.6
  133.4 1.7 constant_dynamic-update-slice_fusion.15
  135.0 1.7 constant_dynamic-update-slice_fusion.14
  136.7 1.7 constant_dynamic-update-slice_fusion.13
  138.4 1.7 constant_dynamic-update-slice_fusion.12
  140.0 0.7 constant_dynamic-update-slice_fusion.11
  140.7 0.7 constant_dynamic-update-slice_fusion.10
  141.5 0.7 constant_dynamic-update-slice_fusion.9
  142.2 0.7 constant_dynamic-update-slice_fusion.8
  142.9 1.7 constant_dynamic-update-slice_fusion.7
  144.6 1.7 constant_dynamic-update-slice_fusion.6
  146.2 1.7 constant_dynamic-update-slice_fusion.5
  147.9 0.7 constant_dynamic-update-slice_fusion.4
  148.6 0.7 constant_dynamic-update-slice_fusion.3
  149.4 0.7 constant_dynamic-update-slice_fusion.2
  150.1 0.7 constant_dynamic-update-slice_fusion.1
  150.8 0.7 constant_dynamic-update-slice_fusion
  151.5 106.4 %all-reduce.5.cloned.1.call-done = f32[512,32]{1,0:T(8,128)} async-done(((f32[512,32]{1,0:T(8,128)}), f32[512,32]{1,0:T(8,128)}) %all-reduce.5.cloned.1.call-update) | async-done | bytes 65552 | tf_op jit(solution)/shard_map/psum | solution.py:34
  257.9 6.3 %multiply_add_fusion = (bf16[2048,512]{0,1:T(8,128)(2,1)}, f32[2048,512]{0,1:T(8,128)S(1)}) fusion(bf16[2048,1024]{0,1:T(8,128)(2,1)} %constant_dynamic-update-slice_fusion, s32[]{:T(128)S(6)} %select_n.21, f32[32,2048]{1,0:T(8,128)S(1)} %fusion.14, f32[512,32]{1,0:T(8,128)} %all-reduce.5.cloned.1.call-done), kind=kOutput, calls=%fused_computation.5 | convolution fusion | flops 406863872 | bytes 8716292 | tf_op jit(solution)/shard_map/dot_general | solution.py:35
  264.2 4.7 %fusion.2 = (bf16[1,2048,512]{1,2,0:T(8,128)(2,1)}, bf16[2048,512]{0,1:T(8,128)(2,1)S(1)}) fusion(f32[2048,512]{0,1:T(8,128)S(1)} %get-tuple-element.11, bf16[1,2048,512]{1,2,0:T(8,128)(2,1)S(1)} %copy-done.3, bf16[1,2048,512]{1,2,0:T(8,128)(2,1)S(1)} %copy-done.1, bf16[2048,512]{0,1:T(8,128)(2,1)S(1)} %copy-done.2, ...), kind=kLoop, calls=%fused_computation.6 | loop fusion | flops 15728640 | bytes 16777220 | tf_op jit(solution)/shard_map/broadcast_in_dim | solution.py:36
  268.9 1.3 copy-done.4
  270.3 2.2 fusion.5
  272.5 0.0 reduce-scatter.2.cloned.1.call-update
  272.5 3.9 %copy.15 = bf16[2048,512]{1,0:T(8,128)(2,1)} copy(bf16[2048,512]{0,1:T(8,128)(2,1)} %copy-done.4) | data formatting | bytes 4194304
  276.5 3.9 %copy.16 = bf16[1,2048,512]{2,1,0:T(8,128)(2,1)} copy(bf16[1,2048,512]{1,2,0:T(8,128)(2,1)} %get-tuple-element.8) | data formatting | bytes 4194304
  280.4 1.7 dynamic-slice_convert_fusion
  282.1 17.6 %reduce-scatter.2.cloned.1.call-done = f32[128,512]{0,1:T(8,128)} async-done(((f32[512,512]{0,1:T(8,128)}), f32[128,512]{0,1:T(8,128)}) %reduce-scatter.2.cloned.1.call-update) | async-done | bytes 262160 | tf_op jit(solution)/shard_map/reduce_scatter | solution.py:46
  299.7 1.0 convert_bitcast_fusion
  300.6 0.8 copy.17
  (16 shorter events, 0.1 us)
Async XLA Ops:
  7.2 263.1 %copy-start = (bf16[1,512,2048]{2,1,0:T(8,128)(2,1)S(1)}, bf16[1,512,2048]{2,1,0:T(8,128)(2,1)}, u32[]{:S(2)}) copy-start(bf16[1,512,2048]{2,1,0:T(8,128)(2,1)} %param.11) | copy-start | bytes 6291460
  7.2 85.2 %all-reduce.3.cloned.1.call-start = ((), (), s32[]{:S(2)}) async-start(), calls=%async_computation.1 | async-start | bytes 524288 | tf_op jit(solution)/shard_map/psum | solution.py:28
  7.2 8.8 %collective-permute-start = (bf16[2048,64]{0,1:T(8,128)(2,1)}, bf16[2048,64]{0,1:T(8,128)(2,1)S(1)}, u32[]{:S(2)}, u32[]{:S(2)}) collective-permute-start(bf16[2048,64]{0,1:T(8,128)(2,1)} %param.8), channel_id=1, source_target_pairs={{0,4},{4,8},{8,12},{12,16},{16,20},{20,24},{24,28},{28,0},{1,5},{5... | collective-permute-start | bytes 786440 | tf_op jit(solution)/shard_map/ppermute | solution.py:16
  16.1 11.8 %collective-permute-start.1 = (bf16[2048,64]{0,1:T(8,128)(2,1)S(1)}, bf16[2048,64]{0,1:T(8,128)(2,1)S(1)}, u32[]{:S(2)}, u32[]{:S(2)}) collective-permute-start(bf16[2048,64]{0,1:T(8,128)(2,1)S(1)} %collective-permute-done), channel_id=1, source_target_pairs={{0,4},{4,8},{8,12},{12,16},{16,20},{20,24},{24,28},{28,0},{1,5},{5... | collective-permute-start | bytes 786440 | tf_op jit(solution)/shard_map/ppermute | solution.py:16
  20.0 8.2 %copy-start.8 = (f32[512,32]{0,1:T(8,128)S(1)}, f32[512,32]{0,1:T(8,128)}, u32[]{:S(2)}) copy-start(f32[512,32]{0,1:T(8,128)} %param.10) | copy-start | bytes 196612
  27.9 7.6 %collective-permute-start.2 = (bf16[2048,64]{0,1:T(8,128)(2,1)S(1)}, bf16[2048,64]{0,1:T(8,128)(2,1)S(1)}, u32[]{:S(2)}, u32[]{:S(2)}) collective-permute-start(bf16[2048,64]{0,1:T(8,128)(2,1)S(1)} %collective-permute-done.1), channel_id=1, source_target_pairs={{0,4},{4,8},{8,12},{12,16},{16,20},{20,24},{24,28},{28,0},{1,5},{5... | collective-permute-start | bytes 786440 | tf_op jit(solution)/shard_map/ppermute | solution.py:16
  35.1 222.9 %all-reduce.5.cloned.1.call-start = ((), (), s32[]{:S(2)}) async-start(), calls=%async_computation.2 | async-start | bytes 524288 | tf_op jit(solution)/shard_map/psum | solution.py:34
  35.5 74.3 %collective-permute-start.3 = (bf16[2048,64]{0,1:T(8,128)(2,1)S(1)}, bf16[2048,64]{0,1:T(8,128)(2,1)S(1)}, u32[]{:S(2)}, u32[]{:S(2)}) collective-permute-start(bf16[2048,64]{0,1:T(8,128)(2,1)S(1)} %collective-permute-done.2), channel_id=1, source_target_pairs={{0,4},{4,8},{8,12},{12,16},{16,20},{20,24},{24,28},{28,0},{1,5},{5... | collective-permute-start | bytes 786440 | tf_op jit(solution)/shard_map/ppermute | solution.py:16
  109.8 8.4 %copy-start.6 = (bf16[2048,64]{0,1:T(8,128)(2,1)}, bf16[2048,64]{0,1:T(8,128)(2,1)S(1)}, u32[]{:S(2)}) copy-start(bf16[2048,64]{0,1:T(8,128)(2,1)S(1)} %collective-permute-done.3) | copy-start | bytes 786436
  109.8 7.7 %collective-permute-start.4 = (bf16[2048,64]{0,1:T(8,128)(2,1)S(1)}, bf16[2048,64]{0,1:T(8,128)(2,1)}, u32[]{:S(2)}, u32[]{:S(2)}) collective-permute-start(bf16[2048,64]{0,1:T(8,128)(2,1)S(1)} %collective-permute-done.3), channel_id=1, source_target_pairs={{0,4},{4,8},{8,12},{12,16},{16,20},{20,24},{24,28},{28,0},{1,5},{5... | collective-permute-start | bytes 786440 | tf_op jit(solution)/shard_map/ppermute | solution.py:16
  117.5 7.9 %collective-permute-start.5 = (bf16[2048,64]{0,1:T(8,128)(2,1)}, bf16[2048,64]{0,1:T(8,128)(2,1)}, u32[]{:S(2)}, u32[]{:S(2)}) collective-permute-start(bf16[2048,64]{0,1:T(8,128)(2,1)} %collective-permute-done.4), channel_id=1, source_target_pairs={{0,4},{4,8},{8,12},{12,16},{16,20},{20,24},{24,28},{28,0},{1,5},{5... | collective-permute-start | bytes 786440 | tf_op jit(solution)/shard_map/ppermute | solution.py:16
  122.0 20.1 %copy-start.5 = (bf16[2048,64]{0,1:T(8,128)(2,1)S(1)}, bf16[2048,64]{0,1:T(8,128)(2,1)}, u32[]{:S(2)}) copy-start(bf16[2048,64]{0,1:T(8,128)(2,1)} %param.8) | copy-start | bytes 786436
  125.4 7.9 %collective-permute-start.6 = (bf16[2048,64]{0,1:T(8,128)(2,1)}, bf16[2048,64]{0,1:T(8,128)(2,1)}, u32[]{:S(2)}, u32[]{:S(2)}) collective-permute-start(bf16[2048,64]{0,1:T(8,128)(2,1)} %collective-permute-done.5), channel_id=1, source_target_pairs={{0,4},{4,8},{8,12},{12,16},{16,20},{20,24},{24,28},{28,0},{1,5},{5... | collective-permute-start | bytes 786440 | tf_op jit(solution)/shard_map/ppermute | solution.py:16
  131.9 167.8 %reduce-scatter.2.cloned.1.call-start = ((), (), s32[]{:S(2)}) async-start(), calls=%async_computation.3 | async-start | bytes 1310720 | tf_op jit(solution)/shard_map/reduce_scatter | solution.py:46
  132.1 15.8 %copy-start.7 = (bf16[2048,64]{0,1:T(8,128)(2,1)S(1)}, bf16[2048,64]{0,1:T(8,128)(2,1)}, u32[]{:S(2)}) copy-start(bf16[2048,64]{0,1:T(8,128)(2,1)} %copy-done.6) | copy-start | bytes 786436
  257.9 6.3 %copy-start.1 = (bf16[1,2048,512]{1,2,0:T(8,128)(2,1)S(1)}, bf16[1,2048,512]{1,2,0:T(8,128)(2,1)}, u32[]{:S(2)}) copy-start(bf16[1,2048,512]{1,2,0:T(8,128)(2,1)} %copy.11) | copy-start | bytes 6291460
  257.9 6.3 %copy-start.2 = (bf16[2048,512]{0,1:T(8,128)(2,1)S(1)}, bf16[2048,512]{0,1:T(8,128)(2,1)}, u32[]{:S(2)}) copy-start(bf16[2048,512]{0,1:T(8,128)(2,1)} %copy.10) | copy-start | bytes 6291460
  257.9 6.3 %copy-start.3 = (bf16[1,2048,512]{1,2,0:T(8,128)(2,1)S(1)}, bf16[1,2048,512]{1,2,0:T(8,128)(2,1)}, u32[]{:S(2)}) copy-start(bf16[1,2048,512]{1,2,0:T(8,128)(2,1)} %copy.12) | copy-start | bytes 6291460
  268.9 1.3 copy-start.4
Sparse Core Ops, SparseCore 0:
  35.2 57.1 all-reduce.2
  132.0 125.9 all-reduce.4
  272.7 26.9 reduce-scatter.1
